TPU v7x, 32 devices: a whole 2x2x4 slice. The times are simulated.
32 devices in a mesh: nest: 4 (over x, core), py: 2 (over y), px: 4 (over z).
Axes of the slice: x: 2, y: 2, z: 4, core: 2. Of those that a mesh axis runs over, the one named last changes fastest.
Arguments:
- initial_state: float32 [4, 4, 256, 256], P('nest', None, 'px', 'py'), may hold values from -6 to 6
- drive_modes: float32 [3, 4, 64, 64], replicated, may hold values from -6 to 6
- relax_rates: float32 [4, 4], P('nest'), may hold values from 0.2 to 0.9
- nest_offsets: int32 [4, 2], replicated, may hold values from 0 to 170
Outputs:
- final_state: float32 [4, 4, 256, 256], P('nest', None, 'px', 'py')
- final_modes: float32 [4, 4, 64, 64], P('nest')
Inputs may be any that keep to these rules, and one draw needn't show every extreme that they name: `nest_offsets`: row 0 is not read.
All inputs are finite; a program needn't handle non-finite values.
Results may differ from a plain program's by a relative error of at most 0.0001.
Values sent between devices are 32-bit elements; how exact they have to be, the bound alone decides.
A program may use at most 64 MiB of HBM per device.

v0:
```python
import math
import jax
import jax.numpy as jnp
import numpy as np
from jax import lax
from jax.sharding import PartitionSpec as P

RATIO = 3
RATE = 0.2
HI = lax.Precision.HIGHEST


def basis(cells, modes, refine, fn=np.cos):
    j = np.arange(modes, dtype=np.int64)
    q = 2 * np.arange(cells, dtype=np.int64) + 1
    product = j[None, :] * q[:, None] % (4 * refine * cells)
    weight = np.where(j == 0, 1.0, 2.0) / cells
    return np.sqrt(weight)[None, :] * fn(np.pi * product / (2.0 * refine * cells))


def half_step(table):
    pad = np.pad(table, ((1, 1), (0, 0)))
    return (0.5 - 2 * RATE) * table + RATE * (pad[2:] + pad[:-2])


def powers(table, count):
    out = [table]
    for _ in range(count):
        out.append(half_step(out[-1]))
    return out


def offset_map(cells, modes, offset):
    base = basis(cells, modes, 1)
    even = jnp.asarray(base.T @ basis(cells, modes, RATIO), jnp.float32)
    odd = jnp.asarray(base.T @ basis(cells, modes, RATIO, np.sin), jnp.float32)
    j = jnp.arange(modes, dtype=jnp.int32)
    product = j * (2 * RATIO * offset) % (4 * RATIO * cells)
    angle = jnp.pi * product.astype(jnp.float32) / (2.0 * RATIO * cells)
    return even * jnp.cos(angle)[None, :] - odd * jnp.sin(angle)[None, :]


def exchange(value, axis, dim, width):
    n, length = (lax.axis_size(axis), value.shape[dim])
    up = [(i, i + 1) for i in range(n - 1)]
    down = [(i + 1, i) for i in range(n - 1)]
    before = lax.ppermute(lax.slice_in_dim(value, length - width, length, axis=dim), axis, up)
    after = lax.ppermute(lax.slice_in_dim(value, 0, width, axis=dim), axis, down)
    return jnp.concatenate([before, value, after], axis=dim)


def free_steps(field, total_x, total_y, steps):
    levels, cx, cy = field.shape
    pad = exchange(exchange(field, "py", 2, steps), "px", 1, steps)
    gx = lax.axis_index("px") * cx - steps + jnp.arange(cx + 2 * steps)
    gy = lax.axis_index("py") * cy - steps + jnp.arange(cy + 2 * steps)
    inside = ((gx >= 0) & (gx < total_x))[:, None] & ((gy >= 0) & (gy < total_y))[None, :]
    for s in range(steps):
        mid = pad[:, 1:-1, 1:-1]
        near = pad[:, 2:, 1:-1] + pad[:, :-2, 1:-1] + pad[:, 1:-1, 2:] + pad[:, 1:-1, :-2]
        pad = mid + RATE * (near - 4.0 * mid)
        cut = s + 1
        pad = jnp.where(inside[cut:-cut, cut:-cut][None], pad, 0.0)
    return pad


def body(initial_state, drive_modes, relax_rates, nest_offsets):
    k = lax.axis_index("nest")
    nests = lax.axis_size("nest")
    field = initial_state[0]
    levels, cx, cy = field.shape
    windows, _, m, _ = drive_modes.shape
    nx, ny = (cx * lax.axis_size("px"), cy * lax.axis_size("py"))
    rp, cp = (powers(basis(nx, m, 1), windows), powers(basis(ny, m, 1), windows))
    a = [jnp.asarray(rp[0].T @ t, jnp.float32) for t in rp]
    b = [jnp.asarray(cp[0].T @ t, jnp.float32) for t in cp]
    u_all = jnp.asarray(np.concatenate(rp, 1), jnp.float32)
    v_all = jnp.asarray(np.concatenate(cp, 1), jnp.float32)
    u = lax.dynamic_slice_in_dim(u_all, lax.axis_index("px") * cx, cx, 0)
    v = lax.dynamic_slice_in_dim(v_all, lax.axis_index("py") * cy, cy, 0)
    half = jnp.einsum("lxy,yq->lxq", field, v, precision=HI)
    rows = []
    for w in range(1, windows + 1):
        terms = [math.comb(w, i) * half[:, :, (w - i) * m : (w - i + 1) * m] for i in range(w + 1)]
        rows.append(
            jnp.einsum(
                "xj,lxm->ljm",
                jnp.concatenate([u[:, i * m : (i + 1) * m] for i in range(w + 1)], 0),
                jnp.concatenate(terms, 1),
                precision=HI,
            )
        )
    shares = lax.psum(jnp.stack(rows), ("py", "px"))
    gain = relax_rates[0][:, None, None]
    row_map = offset_map(nx, m, nest_offsets[k, 0])
    col_map = offset_map(ny, m, nest_offsets[k, 1])

    def left(t, x):
        return jnp.einsum("jp,lpq->ljq", t, x, precision=HI)

    def right(x, t):
        return jnp.einsum("ljq,mq->ljm", x, t, precision=HI)

    def spread(d, x):
        out = left(a[d], x) + right(x, b[d])
        for i in range(1, d):
            out = out + math.comb(d, i) * right(left(a[i], x), b[d - i])
        return out

    parent = jnp.zeros_like(drive_modes)
    for stage in range(nests):
        if stage:
            parent = lax.ppermute(coeffs, "nest", [(i, i + 1) for i in range(nests - 1)])
            interp = jnp.einsum("jp,wlpq->wljq", row_map, parent, precision=HI)
            interp = jnp.einsum("wljq,mq->wljm", interp, col_map, precision=HI)
            target = jnp.where(k == 0, drive_modes, interp)
        else:
            target = drive_modes
        changes, kept = ([], [])
        for w in range(windows):
            own = shares[w]
            for e in range(w):
                own = own + spread(w - e, changes[e])
            changes.append(gain * (target[w] - own))
            kept.append(own + changes[-1])
        coeffs = jnp.stack(kept)
    free = free_steps(field, nx, ny, windows)
    zero = jnp.zeros_like(changes[0])
    blocks = [
        jnp.concatenate(
            [
                math.comb(i + j, i) * changes[windows - 1 - i - j] if i + j < windows else zero
                for j in range(windows)
            ],
            2,
        )
        for i in range(windows)
    ]
    mixed = jnp.concatenate(blocks, 1)
    wide = windows * m
    back = jnp.einsum("lpq,yq->lpy", mixed, v[:, :wide], precision=HI)
    final = free + jnp.einsum("xp,lpy->lxy", u[:, :wide], back, precision=HI)
    return (final[None], coeffs[windows - 1][None])


def solution(mesh):
    spec = P("nest", None, "px", "py")
    return jax.shard_map(
        body,
        mesh=mesh,
        in_specs=(spec, P(), P("nest", None), P()),
        out_specs=(spec, P("nest", None, None, None)),
        check_vma=False,
    )
```

profile of v0, /device:TPU:1, one launch (start us, length us, event | category | flops | bytes accessed | tf_op | source)
XLA Modules:
  0.0 136.2 jit_solution(14306321260385565725)
XLA Ops:
  7.2 1.3 convolution_bitcast_fusion.3
  8.7 0.8 copy-done.7
  10.8 0.8 pad_maximum_fusion
  11.7 0.9 copy-done.3
  12.6 4.1 %collective-permute-start = (f32[4,64,3]{2,1,0:T(8,128)S(1)}, f32[4,64,3]{2,1,0:T(8,128)S(1)}, u32[]{:S(2)}, u32[]{:S(2)}) collective-permute-start(f32[4,64,3]{2,1,0:T(8,128)S(1)} %get-tuple-element.23), channel_id=1, source_target_pairs={{0,4},{1,5},{2,6},{3,7},{8,12},{9,13},{10,14},{11,15},{16,20},{17,... | collective-permute-start | bytes 9224 | tf_op jit(solution)/shard_map/ppermute | solution.py:47
  16.7 1.3 collective-permute-start.1
  18.1 0.7 copy-done.9
  18.8 0.6 constant_dynamic-slice_fusion.2
  20.8 4.1 %collective-permute-done.1 = f32[4,64,3]{2,1,0:T(8,128)S(1)} collective-permute-done((f32[4,64,3]{2,1,0:T(8,128)S(1)}, f32[4,64,3]{2,1,0:T(8,128)S(1)}, u32[]{:S(2)}, u32[]{:S(2)}) %collective-permute-start.1) | collective-permute-done | bytes 3104 | tf_op jit(solution)/shard_map/ppermute | solution.py:48
  25.0 3.2 %collective-permute-start.2 = (f32[4,3,134]{2,1,0:T(4,128)S(1)}, f32[4,3,134]{2,1,0:T(4,128)S(1)}, u32[]{:S(2)}, u32[]{:S(2)}) collective-permute-start(f32[4,3,134]{2,1,0:T(4,128)S(1)} %get-tuple-element.10), channel_id=1, source_target_pairs={{0,1},{1,2},{2,3},{4,5},{5,6},{6,7},{8,9},{9,10},{10,11},{12,13},{... | collective-permute-start | bytes 19304 | tf_op jit(solution)/shard_map/ppermute | solution.py:47
  28.3 1.3 collective-permute-start.3
  29.6 54.6 %all-reduce.3.cloned.1.call-done = f32[3,4,64,64]{3,2,1,0:T(8,128)} async-done(((f32[3,4,64,64]{3,2,1,0:T(8,128)}), f32[3,4,64,64]{3,2,1,0:T(8,128)}) %all-reduce.3.cloned.1.call-update) | async-done | bytes 196624 | tf_op jit(solution)/shard_map/psum | solution.py:93
  84.3 1.0 bitcast_multiply_fusion.2
  88.4 5.6 %collective-permute-start.4 = (f32[3,4,64,64]{3,2,1,0:T(8,128)S(1)}, f32[3,4,64,64]{3,2,1,0:T(8,128)S(1)}, u32[]{:S(2)}, u32[]{:S(2)}) collective-permute-start(f32[3,4,64,64]{3,2,1,0:T(8,128)S(1)} %pad_maximum_fusion.1), channel_id=1, source_target_pairs={{0,8},{8,16},{16,24},{1,9},{9,17},{17,25},{2,10},{10,18},{18,26},{... | collective-permute-start | bytes 589832 | tf_op jit(solution)/shard_map/ppermute | solution.py:113
  94.7 4.1 %collective-permute-done.4 = f32[3,4,64,64]{3,2,1,0:T(8,128)S(1)} collective-permute-done((f32[3,4,64,64]{3,2,1,0:T(8,128)S(1)}, f32[3,4,64,64]{3,2,1,0:T(8,128)S(1)}, u32[]{:S(2)}, u32[]{:S(2)}) %collective-permute-start.4) | collective-permute-done | bytes 196640 | tf_op jit(solution)/shard_map/ppermute | solution.py:113
  98.8 0.5 convolution_bitcast_fusion.2
  102.2 4.4 %collective-permute-start.5 = (f32[3,4,64,64]{3,2,1,0:T(8,128)S(1)}, f32[3,4,64,64]{3,2,1,0:T(8,128)S(1)}, u32[]{:S(2)}, u32[]{:S(2)}) collective-permute-start(f32[3,4,64,64]{3,2,1,0:T(8,128)S(1)} %pad_maximum_fusion.2), channel_id=1, source_target_pairs={{0,8},{8,16},{16,24},{1,9},{9,17},{17,25},{2,10},{10,18},{18,26},{... | collective-permute-start | bytes 589832 | tf_op jit(solution)/shard_map/ppermute | solution.py:113
  107.0 4.3 %collective-permute-done.5 = f32[3,4,64,64]{3,2,1,0:T(8,128)S(1)} collective-permute-done((f32[3,4,64,64]{3,2,1,0:T(8,128)S(1)}, f32[3,4,64,64]{3,2,1,0:T(8,128)S(1)}, u32[]{:S(2)}, u32[]{:S(2)}) %collective-permute-start.5) | collective-permute-done | bytes 196640 | tf_op jit(solution)/shard_map/ppermute | solution.py:113
  111.3 0.5 convolution_bitcast_fusion.1
  114.8 4.6 %collective-permute-start.6 = (f32[3,4,64,64]{3,2,1,0:T(8,128)S(1)}, f32[3,4,64,64]{3,2,1,0:T(8,128)S(1)}, u32[]{:S(2)}, u32[]{:S(2)}) collective-permute-start(f32[3,4,64,64]{3,2,1,0:T(8,128)S(1)} %pad_maximum_fusion.3), channel_id=1, source_target_pairs={{0,8},{8,16},{16,24},{1,9},{9,17},{17,25},{2,10},{10,18},{18,26},{... | collective-permute-start | bytes 589832 | tf_op jit(solution)/shard_map/ppermute | solution.py:113
  119.8 4.1 %collective-permute-done.6 = f32[3,4,64,64]{3,2,1,0:T(8,128)S(1)} collective-permute-done((f32[3,4,64,64]{3,2,1,0:T(8,128)S(1)}, f32[3,4,64,64]{3,2,1,0:T(8,128)S(1)}, u32[]{:S(2)}, u32[]{:S(2)}) %collective-permute-start.6) | collective-permute-done | bytes 196640 | tf_op jit(solution)/shard_map/ppermute | solution.py:113
  126.6 0.9 add_bitcast_fusion
  127.5 0.8 fusion.20
  128.4 1.0 fusion.1
  (83 shorter events, 14.6 us)
Async XLA Ops:
  7.2 77.1 %all-reduce.3.cloned.1.call-start = ((), (), s32[]{:S(2)}) async-start(), calls=%async_computation | async-start | bytes 786432 | tf_op jit(solution)/shard_map/psum | solution.py:93
  8.6 1.0 copy-start.7
  11.6 0.9 copy-start.3
  12.5 71.7 %copy-start.1 = (f32[3,4,64,64]{3,2,1,0:T(8,128)S(1)}, f32[3,4,64,64]{3,2,1,0:T(8,128)}, u32[]{:S(2)}) copy-start(f32[3,4,64,64]{3,2,1,0:T(8,128)} %param.15) | copy-start | bytes 589828
  12.6 8.2 %collective-permute-start = (f32[4,64,3]{2,1,0:T(8,128)S(1)}, f32[4,64,3]{2,1,0:T(8,128)S(1)}, u32[]{:S(2)}, u32[]{:S(2)}) collective-permute-start(f32[4,64,3]{2,1,0:T(8,128)S(1)} %get-tuple-element.23), channel_id=1, source_target_pairs={{0,4},{1,5},{2,6},{3,7},{8,12},{9,13},{10,14},{11,15},{16,20},{17,... | collective-permute-start | bytes 9224 | tf_op jit(solution)/shard_map/ppermute | solution.py:47
  16.7 8.2 %collective-permute-start.1 = (f32[4,64,3]{2,1,0:T(8,128)S(1)}, f32[4,64,3]{2,1,0:T(8,128)S(1)}, u32[]{:S(2)}, u32[]{:S(2)}) collective-permute-start(f32[4,64,3]{2,1,0:T(8,128)S(1)} %get-tuple-element.24), channel_id=1, source_target_pairs={{4,0},{5,1},{6,2},{7,3},{12,8},{13,9},{14,10},{15,11},{20,16},{21,... | collective-permute-start | bytes 9224 | tf_op jit(solution)/shard_map/ppermute | solution.py:48
  18.1 0.7 copy-start.9
  25.0 69.4 %collective-permute-start.2 = (f32[4,3,134]{2,1,0:T(4,128)S(1)}, f32[4,3,134]{2,1,0:T(4,128)S(1)}, u32[]{:S(2)}, u32[]{:S(2)}) collective-permute-start(f32[4,3,134]{2,1,0:T(4,128)S(1)} %get-tuple-element.10), channel_id=1, source_target_pairs={{0,1},{1,2},{2,3},{4,5},{5,6},{6,7},{8,9},{9,10},{10,11},{12,13},{... | collective-permute-start | bytes 19304 | tf_op jit(solution)/shard_map/ppermute | solution.py:47
  28.3 56.0 %copy-start.8 = (f32[1,4]{1,0:T(1,128)S(1)}, f32[1,4]{1,0:T(1,128)}, u32[]{:S(2)}) copy-start(f32[1,4]{1,0:T(1,128)} %param.16) | copy-start | bytes 52
  28.3 66.2 %collective-permute-start.3 = (f32[4,3,134]{2,1,0:T(4,128)S(1)}, f32[4,3,134]{2,1,0:T(4,128)S(1)}, u32[]{:S(2)}, u32[]{:S(2)}) collective-permute-start(f32[4,3,134]{2,1,0:T(4,128)S(1)} %get-tuple-element.11), channel_id=1, source_target_pairs={{1,0},{2,1},{3,2},{5,4},{6,5},{7,6},{9,8},{10,9},{11,10},{13,12},{... | collective-permute-start | bytes 19304 | tf_op jit(solution)/shard_map/ppermute | solution.py:48
  84.3 1.0 copy-start
  85.3 1.0 copy-start.2
  87.0 0.8 copy-start.4
  88.4 10.3 %collective-permute-start.4 = (f32[3,4,64,64]{3,2,1,0:T(8,128)S(1)}, f32[3,4,64,64]{3,2,1,0:T(8,128)S(1)}, u32[]{:S(2)}, u32[]{:S(2)}) collective-permute-start(f32[3,4,64,64]{3,2,1,0:T(8,128)S(1)} %pad_maximum_fusion.1), channel_id=1, source_target_pairs={{0,8},{8,16},{16,24},{1,9},{9,17},{17,25},{2,10},{10,18},{18,26},{... | collective-permute-start | bytes 589832 | tf_op jit(solution)/shard_map/ppermute | solution.py:113
  94.4 4.3 %copy-start.5 = (f32[64,64]{1,0:T(8,128)S(1)}, f32[64,64]{1,0:T(8,128)}, u32[]{:S(2)}) copy-start(f32[64,64]{1,0:T(8,128)} %constant.86.clone) | copy-start | bytes 49156
  94.5 4.3 %copy-start.6 = (f32[64,64]{1,0:T(8,128)S(1)}, f32[64,64]{1,0:T(8,128)}, u32[]{:S(2)}) copy-start(f32[64,64]{1,0:T(8,128)} %constant.87.clone) | copy-start | bytes 49156
  102.2 9.1 %collective-permute-start.5 = (f32[3,4,64,64]{3,2,1,0:T(8,128)S(1)}, f32[3,4,64,64]{3,2,1,0:T(8,128)S(1)}, u32[]{:S(2)}, u32[]{:S(2)}) collective-permute-start(f32[3,4,64,64]{3,2,1,0:T(8,128)S(1)} %pad_maximum_fusion.2), channel_id=1, source_target_pairs={{0,8},{8,16},{16,24},{1,9},{9,17},{17,25},{2,10},{10,18},{18,26},{... | collective-permute-start | bytes 589832 | tf_op jit(solution)/shard_map/ppermute | solution.py:113
  114.8 9.1 %collective-permute-start.6 = (f32[3,4,64,64]{3,2,1,0:T(8,128)S(1)}, f32[3,4,64,64]{3,2,1,0:T(8,128)S(1)}, u32[]{:S(2)}, u32[]{:S(2)}) collective-permute-start(f32[3,4,64,64]{3,2,1,0:T(8,128)S(1)} %pad_maximum_fusion.3), channel_id=1, source_target_pairs={{0,8},{8,16},{16,24},{1,9},{9,17},{17,25},{2,10},{10,18},{18,26},{... | collective-permute-start | bytes 589832 | tf_op jit(solution)/shard_map/ppermute | solution.py:113
Sparse Core Ops, SparseCore 0:
  11.8 72.4 all-reduce.2
where the time goes:
time: 137 us; the launch traced here: 136 us
  waiting for transfers between devices  71.3 us (52%)
  starting transfers between devices  24.6 us (18%)
  matrix products  16.2 us (12%)
  between operations  16 us (12%)
  local copies, waits for them, and re-layouts  4.31 us (3%)
  other arithmetic  3.84 us (3%)
    psum x1, waiting for transfers between devices, body(): shares = lax.psum(jnp.stack(rows), ('py', 'px'))  54.6 us
    ppermute x3, starting transfers between devices, body(): lax.ppermute(coeffs, 'nest', [(i, i + 1) for i in range(nests - 1)])  14.6 us
    ppermute x3, waiting for transfers between devices, body(): lax.ppermute(coeffs, 'nest', [(i, i + 1) for i in range(nests - 1)])  12.5 us
    ppermute x2, starting transfers between devices, exchange(): lax.ppermute(lax.slice_in_dim(value, length - width, length, axis=dim), a...  7.35 us
    dot_general x16, matrix products, right(): return jnp.einsum('ljq,mq->ljm', x, t, precision=HI)  5.31 us
    ppermute x2, waiting for transfers between devices, exchange(): lax.ppermute(lax.slice_in_dim(value, 0, width, axis=dim), axis, down)  4.13 us
    dot_general x12, matrix products, left(): return jnp.einsum('jp,lpq->ljq', t, x, precision=HI)  3.66 us
    unnamed x20, local copies, waits for them, and re-layouts  3.27 us
  transfers between devices with their start and end apart: 8, of which 5 were waited for; matrix products, arithmetic and copies ran while one was open for 4% of the time, Pallas kernels for 0%

commit v1 on v0

--- a/solution.py
+++ b/solution.py
@@ -90,7 +90,7 @@
                 precision=HI,
             )
         )
-    shares = lax.psum(jnp.stack(rows), ("py", "px"))
+    shares = jnp.sum(lax.all_gather(jnp.stack(rows), ("py", "px")), axis=0)
     gain = relax_rates[0][:, None, None]
     row_map = offset_map(nx, m, nest_offsets[k, 0])
     col_map = offset_map(ny, m, nest_offsets[k, 1])

time: 137 us -> 127 us (0.927)
  waiting for transfers between devices: 71.3 us -> 61.6 us
  local copies, waits for them, and re-layouts: 4.31 us -> 2.88 us
    psum x1 -> x0, waiting for transfers between devices: 54.6 us -> none  [body(): shares = lax.psum(jnp.stack(rows), ('py', 'px'))]
    all_gather x0 -> x1, waiting for transfers between devices: none -> 46.7 us  [body(): shares = jnp.sum(lax.all_gather(jnp.stack(rows), ('py', 'px')), axis=0)]
    unnamed x20 -> x18, local copies, waits for them, and re-layouts: 3.27 us -> 0.05 us
    reduce_sum x0 -> x1, other arithmetic: none -> 2.28 us  [body(): shares = jnp.sum(lax.all_gather(jnp.stack(rows), ('py', 'px')), axis=0)]
    ppermute x2, waiting for transfers between devices: 4.13 us -> 2.31 us  [exchange(): lax.ppermute(lax.slice_in_dim(value, 0, width, axis=dim), axis, down)]
  transfers between devices with their start and end apart: 8 -> 8, of which waited for: 5 -> 5; matrix products, arithmetic and copies ran while one was open for 4% -> 5% of each run, Pallas kernels for 0% -> 0%
where the time goes in v1:
time: 127 us
  waiting for transfers between devices  61.6 us (49%)
  starting transfers between devices  24.2 us (19%)
  matrix products  17.5 us (14%)
  between operations  16 us (13%)
  other arithmetic  4.44 us (3%)
  local copies, waits for them, and re-layouts  2.88 us (2%)
    all_gather x1, waiting for transfers between devices, body(): shares = jnp.sum(lax.all_gather(jnp.stack(rows), ('py', 'px')), axis=0)  46.7 us
    ppermute x3, starting transfers between devices, body(): lax.ppermute(coeffs, 'nest', [(i, i + 1) for i in range(nests - 1)])  14.4 us
    ppermute x3, waiting for transfers between devices, body(): lax.ppermute(coeffs, 'nest', [(i, i + 1) for i in range(nests - 1)])  12.6 us
    ppermute x2, starting transfers between devices, exchange(): lax.ppermute(lax.slice_in_dim(value, length - width, length, axis=dim), a...  7.15 us
    dot_general x16, matrix products, right(): return jnp.einsum('ljq,mq->ljm', x, t, precision=HI)  5.31 us
    dot_general x12, matrix products, left(): return jnp.einsum('jp,lpq->ljq', t, x, precision=HI)  3.68 us
    ppermute x2, starting transfers between devices, exchange(): lax.ppermute(lax.slice_in_dim(value, 0, width, axis=dim), axis, down)  2.58 us
  transfers between devices with their start and end apart: 8, of which 5 were waited for; matrix products, arithmetic and copies ran while one was open for 5% of the time, Pallas kernels for 0%

profile of v1, /device:TPU:1, one launch (start us, length us, event | category | flops | bytes accessed | tf_op | source)
XLA Modules:
  0.0 126.6 jit_solution(2207021630502635592)
XLA Ops:
  7.2 1.4 %convolution_bitcast_fusion.3 = f32[4,64,256]{2,1,0:T(8,128)S(1)} fusion(f32[256,256]{1,0:T(8,128)} %constant.85.clone, s32[]{:T(128)S(6)} %select_n.67, f32[1,4,64,128]{3,2,1,0:T(8,128)} %param.14), kind=kOutput, calls=%fused_computation.6 | convolution fusion | flops 100663296 | bytes 524292 | tf_op jit(solution)/shard_map/lxy,yq->lxq/dot_general | solution.py:81
  8.8 1.0 constant_dynamic-slice_fusion
  9.7 0.6 convolution_bitcast_fusion.19
  10.3 0.8 convolution_bitcast_fusion.6
  11.1 1.0 convolution_bitcast_fusion.5
  12.2 0.9 copy.46
  13.3 4.0 %collective-permute-start = (f32[4,64,3]{2,1,0:T(8,128)S(1)}, f32[4,64,3]{2,1,0:T(8,128)S(1)}, u32[]{:S(2)}, u32[]{:S(2)}) collective-permute-start(f32[4,64,3]{2,1,0:T(8,128)S(1)} %get-tuple-element.23), channel_id=1, source_target_pairs={{0,4},{1,5},{2,6},{3,7},{8,12},{9,13},{10,14},{11,15},{16,20},{17,... | collective-permute-start | bytes 9224 | tf_op jit(solution)/shard_map/ppermute | solution.py:47
  17.2 1.3 %collective-permute-start.1 = (f32[4,64,3]{2,1,0:T(8,128)S(1)}, f32[4,64,3]{2,1,0:T(8,128)S(1)}, u32[]{:S(2)}, u32[]{:S(2)}) collective-permute-start(f32[4,64,3]{2,1,0:T(8,128)S(1)} %get-tuple-element.24), channel_id=1, source_target_pairs={{4,0},{5,1},{6,2},{7,3},{12,8},{13,9},{14,10},{15,11},{20,16},{21,... | collective-permute-start | bytes 9224 | tf_op jit(solution)/shard_map/ppermute | solution.py:48
  18.5 0.6 constant_dynamic-slice_fusion.2
  20.6 2.3 %collective-permute-done.1 = f32[4,64,3]{2,1,0:T(8,128)S(1)} collective-permute-done((f32[4,64,3]{2,1,0:T(8,128)S(1)}, f32[4,64,3]{2,1,0:T(8,128)S(1)}, u32[]{:S(2)}, u32[]{:S(2)}) %collective-permute-start.1) | collective-permute-done | bytes 3104 | tf_op jit(solution)/shard_map/ppermute | solution.py:48
  23.0 3.2 %collective-permute-start.2 = (f32[4,3,134]{2,1,0:T(4,128)S(1)}, f32[4,3,134]{2,1,0:T(4,128)S(1)}, u32[]{:S(2)}, u32[]{:S(2)}) collective-permute-start(f32[4,3,134]{2,1,0:T(4,128)S(1)} %get-tuple-element.10), channel_id=1, source_target_pairs={{0,1},{1,2},{2,3},{4,5},{5,6},{6,7},{8,9},{9,10},{10,11},{12,13},{... | collective-permute-start | bytes 19304 | tf_op jit(solution)/shard_map/ppermute | solution.py:47
  26.2 1.3 %collective-permute-start.3 = (f32[4,3,134]{2,1,0:T(4,128)S(1)}, f32[4,3,134]{2,1,0:T(4,128)S(1)}, u32[]{:S(2)}, u32[]{:S(2)}) collective-permute-start(f32[4,3,134]{2,1,0:T(4,128)S(1)} %get-tuple-element.11), channel_id=1, source_target_pairs={{1,0},{2,1},{3,2},{5,4},{6,5},{7,6},{9,8},{10,9},{11,10},{13,12},{... | collective-permute-start | bytes 19304 | tf_op jit(solution)/shard_map/ppermute | solution.py:48
  27.5 46.7 %all-gather.3.cloned.1.call-done = f32[24,4,64,64]{3,2,1,0:T(8,128)} async-done(((f32[3,4,64,64]{3,2,1,0:T(8,128)}), f32[24,4,64,64]{3,2,1,0:T(8,128)}) %all-gather.3.cloned.1.call-update) | async-done | bytes 1572880 | tf_op jit(solution)/shard_map/all_gather | solution.py:93
  74.2 2.3 %reduce_sum.9 = f32[3,4,64,64]{3,2,1,0:T(8,128)S(1)} reduce(f32[8,3,4,64,64]{4,3,2,1,0:T(8,128)} %bitcast.271, f32[]{:T(128)} %constant.37.clone.1), dimensions={0}, to_apply=%region_0.0 | reduce | flops 344064 | bytes 1769476 | tf_op jit(solution)/shard_map/reduce_sum | solution.py:93
  78.9 5.4 %collective-permute-start.4 = (f32[3,4,64,64]{3,2,1,0:T(8,128)S(1)}, f32[3,4,64,64]{3,2,1,0:T(8,128)S(1)}, u32[]{:S(2)}, u32[]{:S(2)}) collective-permute-start(f32[3,4,64,64]{3,2,1,0:T(8,128)S(1)} %pad_maximum_fusion.1), channel_id=1, source_target_pairs={{0,8},{8,16},{16,24},{1,9},{9,17},{17,25},{2,10},{10,18},{18,26},{... | collective-permute-start | bytes 589832 | tf_op jit(solution)/shard_map/ppermute | solution.py:113
  84.9 4.1 %collective-permute-done.4 = f32[3,4,64,64]{3,2,1,0:T(8,128)S(1)} collective-permute-done((f32[3,4,64,64]{3,2,1,0:T(8,128)S(1)}, f32[3,4,64,64]{3,2,1,0:T(8,128)S(1)}, u32[]{:S(2)}, u32[]{:S(2)}) %collective-permute-start.4) | collective-permute-done | bytes 196640 | tf_op jit(solution)/shard_map/ppermute | solution.py:113
  89.1 0.5 convolution_bitcast_fusion.2
  92.5 4.4 %collective-permute-start.5 = (f32[3,4,64,64]{3,2,1,0:T(8,128)S(1)}, f32[3,4,64,64]{3,2,1,0:T(8,128)S(1)}, u32[]{:S(2)}, u32[]{:S(2)}) collective-permute-start(f32[3,4,64,64]{3,2,1,0:T(8,128)S(1)} %pad_maximum_fusion.2), channel_id=1, source_target_pairs={{0,8},{8,16},{16,24},{1,9},{9,17},{17,25},{2,10},{10,18},{18,26},{... | collective-permute-start | bytes 589832 | tf_op jit(solution)/shard_map/ppermute | solution.py:113
  97.3 4.3 %collective-permute-done.5 = f32[3,4,64,64]{3,2,1,0:T(8,128)S(1)} collective-permute-done((f32[3,4,64,64]{3,2,1,0:T(8,128)S(1)}, f32[3,4,64,64]{3,2,1,0:T(8,128)S(1)}, u32[]{:S(2)}, u32[]{:S(2)}) %collective-permute-start.5) | collective-permute-done | bytes 196640 | tf_op jit(solution)/shard_map/ppermute | solution.py:113
  105.1 4.6 %collective-permute-start.6 = (f32[3,4,64,64]{3,2,1,0:T(8,128)S(1)}, f32[3,4,64,64]{3,2,1,0:T(8,128)S(1)}, u32[]{:S(2)}, u32[]{:S(2)}) collective-permute-start(f32[3,4,64,64]{3,2,1,0:T(8,128)S(1)} %pad_maximum_fusion.3), channel_id=1, source_target_pairs={{0,8},{8,16},{16,24},{1,9},{9,17},{17,25},{2,10},{10,18},{18,26},{... | collective-permute-start | bytes 589832 | tf_op jit(solution)/shard_map/ppermute | solution.py:113
  110.1 4.1 %collective-permute-done.6 = f32[3,4,64,64]{3,2,1,0:T(8,128)S(1)} collective-permute-done((f32[3,4,64,64]{3,2,1,0:T(8,128)S(1)}, f32[3,4,64,64]{3,2,1,0:T(8,128)S(1)}, u32[]{:S(2)}, u32[]{:S(2)}) %collective-permute-start.6) | collective-permute-done | bytes 196640 | tf_op jit(solution)/shard_map/ppermute | solution.py:113
  116.9 0.9 add_bitcast_fusion
  117.9 0.8 fusion.20
  118.7 1.0 fusion.1
  (83 shorter events, 13.1 us)
Async XLA Ops:
  7.2 67.1 %all-gather.3.cloned.1.call-start = ((), (), s32[]{:S(2)}) async-start(), calls=%async_computation | async-start | bytes 3538944 | tf_op jit(solution)/shard_map/all_gather | solution.py:93
  7.2 5.9 %copy-start.2 = (f32[1,4,64,128]{3,2,1,0:T(8,128)S(1)}, f32[1,4,64,128]{3,2,1,0:T(8,128)}, u32[]{:S(2)}) copy-start(f32[1,4,64,128]{3,2,1,0:T(8,128)} %param.14) | copy-start | bytes 393220
  8.6 9.9 %copy-start.8 = (s32[4,2]{0,1:T(2,128)S(1)}, s32[4,2]{0,1:T(2,128)}, u32[]{:S(2)}) copy-start(s32[4,2]{0,1:T(2,128)} %param.17) | copy-start | bytes 100
  12.1 64.4 %copy-start.1 = (f32[3,4,64,64]{3,2,1,0:T(8,128)S(1)}, f32[3,4,64,64]{3,2,1,0:T(8,128)}, u32[]{:S(2)}) copy-start(f32[3,4,64,64]{3,2,1,0:T(8,128)} %param.15) | copy-start | bytes 589828
  12.2 64.4 %copy-start.7 = (f32[1,4]{1,0:T(1,128)S(1)}, f32[1,4]{1,0:T(1,128)}, u32[]{:S(2)}) copy-start(f32[1,4]{1,0:T(1,128)} %param.16) | copy-start | bytes 52
  12.2 64.4 %copy-start = (f32[64,64,1]{1,0,2:T(8,128)S(1)}, f32[64,64,1]{1,0,2:T(8,128)}, u32[]{:S(2)}) copy-start(f32[64,64,1]{1,0,2:T(8,128)} %constant.92) | copy-start | bytes 49156
  13.3 7.4 %collective-permute-start = (f32[4,64,3]{2,1,0:T(8,128)S(1)}, f32[4,64,3]{2,1,0:T(8,128)S(1)}, u32[]{:S(2)}, u32[]{:S(2)}) collective-permute-start(f32[4,64,3]{2,1,0:T(8,128)S(1)} %get-tuple-element.23), channel_id=1, source_target_pairs={{0,4},{1,5},{2,6},{3,7},{8,12},{9,13},{10,14},{11,15},{16,20},{17,... | collective-permute-start | bytes 9224 | tf_op jit(solution)/shard_map/ppermute | solution.py:47
  17.2 5.7 %collective-permute-start.1 = (f32[4,64,3]{2,1,0:T(8,128)S(1)}, f32[4,64,3]{2,1,0:T(8,128)S(1)}, u32[]{:S(2)}, u32[]{:S(2)}) collective-permute-start(f32[4,64,3]{2,1,0:T(8,128)S(1)} %get-tuple-element.24), channel_id=1, source_target_pairs={{4,0},{5,1},{6,2},{7,3},{12,8},{13,9},{14,10},{15,11},{20,16},{21,... | collective-permute-start | bytes 9224 | tf_op jit(solution)/shard_map/ppermute | solution.py:48
  23.0 61.7 %collective-permute-start.2 = (f32[4,3,134]{2,1,0:T(4,128)S(1)}, f32[4,3,134]{2,1,0:T(4,128)S(1)}, u32[]{:S(2)}, u32[]{:S(2)}) collective-permute-start(f32[4,3,134]{2,1,0:T(4,128)S(1)} %get-tuple-element.10), channel_id=1, source_target_pairs={{0,1},{1,2},{2,3},{4,5},{5,6},{6,7},{8,9},{9,10},{10,11},{12,13},{... | collective-permute-start | bytes 19304 | tf_op jit(solution)/shard_map/ppermute | solution.py:47
  26.2 58.5 %collective-permute-start.3 = (f32[4,3,134]{2,1,0:T(4,128)S(1)}, f32[4,3,134]{2,1,0:T(4,128)S(1)}, u32[]{:S(2)}, u32[]{:S(2)}) collective-permute-start(f32[4,3,134]{2,1,0:T(4,128)S(1)} %get-tuple-element.11), channel_id=1, source_target_pairs={{1,0},{2,1},{3,2},{5,4},{6,5},{7,6},{9,8},{10,9},{11,10},{13,12},{... | collective-permute-start | bytes 19304 | tf_op jit(solution)/shard_map/ppermute | solution.py:48
  74.2 4.1 %copy-start.3 = (f32[64,64,1]{1,0,2:T(8,128)S(1)}, f32[64,64,1]{1,0,2:T(8,128)}, u32[]{:S(2)}) copy-start(f32[64,64,1]{1,0,2:T(8,128)} %constant.93) | copy-start | bytes 49156
  76.5 12.5 %copy-start.4 = (f32[64,64]{1,0:T(8,128)S(1)}, f32[64,64]{1,0:T(8,128)}, u32[]{:S(2)}) copy-start(f32[64,64]{1,0:T(8,128)} %constant.86.clone) | copy-start | bytes 49156
  76.5 12.5 %copy-start.5 = (f32[64,64]{1,0:T(8,128)S(1)}, f32[64,64]{1,0:T(8,128)}, u32[]{:S(2)}) copy-start(f32[64,64]{1,0:T(8,128)} %constant.87.clone) | copy-start | bytes 49156
  78.9 10.1 %collective-permute-start.4 = (f32[3,4,64,64]{3,2,1,0:T(8,128)S(1)}, f32[3,4,64,64]{3,2,1,0:T(8,128)S(1)}, u32[]{:S(2)}, u32[]{:S(2)}) collective-permute-start(f32[3,4,64,64]{3,2,1,0:T(8,128)S(1)} %pad_maximum_fusion.1), channel_id=1, source_target_pairs={{0,8},{8,16},{16,24},{1,9},{9,17},{17,25},{2,10},{10,18},{18,26},{... | collective-permute-start | bytes 589832 | tf_op jit(solution)/shard_map/ppermute | solution.py:113
  92.5 9.1 %collective-permute-start.5 = (f32[3,4,64,64]{3,2,1,0:T(8,128)S(1)}, f32[3,4,64,64]{3,2,1,0:T(8,128)S(1)}, u32[]{:S(2)}, u32[]{:S(2)}) collective-permute-start(f32[3,4,64,64]{3,2,1,0:T(8,128)S(1)} %pad_maximum_fusion.2), channel_id=1, source_target_pairs={{0,8},{8,16},{16,24},{1,9},{9,17},{17,25},{2,10},{10,18},{18,26},{... | collective-permute-start | bytes 589832 | tf_op jit(solution)/shard_map/ppermute | solution.py:113
  105.1 9.1 %collective-permute-start.6 = (f32[3,4,64,64]{3,2,1,0:T(8,128)S(1)}, f32[3,4,64,64]{3,2,1,0:T(8,128)S(1)}, u32[]{:S(2)}, u32[]{:S(2)}) collective-permute-start(f32[3,4,64,64]{3,2,1,0:T(8,128)S(1)} %pad_maximum_fusion.3), channel_id=1, source_target_pairs={{0,8},{8,16},{16,24},{1,9},{9,17},{17,25},{2,10},{10,18},{18,26},{... | collective-permute-start | bytes 589832 | tf_op jit(solution)/shard_map/ppermute | solution.py:113
  110.1 7.8 %copy-start.6 = (f32[256,256]{1,0:T(8,128)S(1)}, f32[256,256]{1,0:T(8,128)}, u32[]{:S(2)}) copy-start(f32[256,256]{1,0:T(8,128)} %constant.85.clone) | copy-start | bytes 786436
Sparse Core Ops, SparseCore 0:
  13.3 60.9 all-gather.2
